TPU v7x, 32 devices: a whole 2x2x4 slice. The times are simulated.
32 devices in a mesh: grp: 4 (over y, x), row: 2 (over core), col: 4 (over z).
Axes of the slice: x: 2, y: 2, z: 4, core: 2. Of those that a mesh axis runs over, the one named last changes fastest.
Arguments:
- normals: float32 [4, 4096, 4096], P('grp', 'row', 'col'), as said below
- transforms: float32 [4, 32, 128, 128], P('grp', 'row'), as said below
- block_map: int32 [4, 32], P('grp'), may hold values from 0 to 31, as said below
Outputs:
- eliminated: float32 [4096, 4096], P('row', 'col')
Inputs may be any that keep to these rules, and one draw needn't show every extreme that they name: `block_map`: for each group, a permutation of the blocks that maps every aligned range of 8 blocks onto itself. `normals`: each group's matrix is symmetric positive definite. `transforms`: each block is nonsingular.
All inputs are finite; a program needn't handle non-finite values.
Results may differ from a plain program's by a relative error of at most 0.0001.
Values sent between devices are 32-bit elements; how exact they have to be, the bound alone decides.
No kernel may reach another device: no remote copies, remote signals or barrier semaphores. Data moves between devices by JAX's collectives and lax.ppermute only.
A program may use at most 64 MiB of HBM per device.

v0:
```python
import jax
import jax.numpy as jnp
from jax import lax
from jax.sharding import PartitionSpec as P

BLK = 128
NPAN = 5


def spread(block, axis, holder):
    block = jnp.where(lax.axis_index(axis) == holder, block, jnp.zeros_like(block))
    return lax.psum(block, axis)


def on_device(normals, transforms, block_map):
    local = normals[0]
    height, width = local.shape
    row_blocks = height // BLK
    col_blocks = width // BLK
    row_index = lax.axis_index("row")
    col_index = lax.axis_index("col")
    row_transforms = transforms[0]
    every_block = lax.all_gather(transforms, "row", axis=1, tiled=True)[0]
    col_transforms = lax.dynamic_slice_in_dim(every_block, col_index * col_blocks, col_blocks, 0)
    grid = local.reshape(row_blocks, BLK, col_blocks, BLK)
    half_done = jnp.einsum("aij,aibk->ajbk", row_transforms, grid, precision=lax.Precision.HIGHEST)
    rotated = jnp.einsum(
        "ajbk,bkl->ajbl", half_done, col_transforms, precision=lax.Precision.HIGHEST
    )
    mapping = block_map[0]
    row_map = (
        lax.dynamic_slice_in_dim(mapping, row_index * row_blocks, row_blocks, 0)
        - row_index * row_blocks
    )
    col_map = (
        lax.dynamic_slice_in_dim(mapping, col_index * col_blocks, col_blocks, 0)
        - col_index * col_blocks
    )
    rotated = jnp.take(rotated, row_map, axis=0)
    rotated = jnp.take(rotated, col_map, axis=2).reshape(height, width)
    matrix = lax.psum(rotated, "grp")
    row_offset = row_index * height
    own_count = matrix.shape[0]
    order_all = height * lax.axis_size("row")
    col_offset = col_index * width
    for panel in range(NPAN):
        offset = panel * BLK
        holder = offset // width
        inside = offset - holder * width
        panel_piece = spread(matrix[:, inside : inside + BLK], "col", holder)
        column = lax.all_gather(panel_piece, "row", axis=0, tiled=True)
        factor_block = jnp.linalg.cholesky(column[offset : offset + BLK])
        factor = lax.linalg.triangular_solve(
            factor_block, column, left_side=False, lower=True, transpose_a=True
        )
        below = jnp.arange(order_all)[:, None] >= offset
        factor = jnp.where(below, factor, jnp.zeros_like(factor))
        own_rows = lax.dynamic_slice_in_dim(factor, row_offset, own_count, 0)
        col_rows = lax.dynamic_slice_in_dim(factor, col_offset, width, 0)
        matrix = matrix - jnp.dot(
            own_rows,
            col_rows.T,
            precision=lax.Precision.HIGHEST,
            preferred_element_type=jnp.float32,
        )
        current = matrix[:, inside : inside + BLK]
        matrix = matrix.at[:, inside : inside + BLK].set(
            jnp.where(col_index == holder, own_rows, current)
        )
    return matrix


def solution(mesh):
    return jax.shard_map(
        on_device,
        mesh=mesh,
        in_specs=(P("grp", "row", "col"), P("grp", "row", None, None), P("grp", None)),
        out_specs=P("row", "col"),
        check_vma=False,
    )
```

profile of v0, /device:TPU:0, one launch (start us, length us, event | category | flops | bytes accessed | tf_op | source)
XLA Modules:
  0.0 811.8 jit_solution(7198959561113941672)
XLA Ops:
  7.3 9.0 %copy.38 = f32[256,8,8,128]{3,2,1,0:T(8,128)} copy(f32[256,8,8,128]{3,1,2,0:T(8,128)} %bitcast.111) | data formatting | bytes 16777216
  16.7 14.3 %fusion = f32[16,128,8,128]{3,1,0,2:T(8,128)} fusion(f32[16,128,8,128]{3,2,1,0:T(8,128)} %bitcast.108, f32[1,16,128,128]{3,2,1,0:T(8,128)S(1)} %copy-done.4), kind=kOutput, calls=%fused_computation.3 | convolution fusion | flops 3221225472 | bytes 17825792 | tf_op jit(solution)/shard_map/aij,aibk->ajbk/dot_general | solution.py:26
  31.0 12.0 %convolution_bitcast_fusion.5 = f32[16,128,8,128]{1,3,0,2:T(8,128)} fusion(f32[16,128,8,128]{3,1,0,2:T(8,128)} %fusion, f32[1,32,128,128]{3,2,0,1:T(8,128)} %all-gather.7.cloned.1.call-done, s32[]{:T(128)S(6)} %select_n.123), kind=kOutput, calls=%fused_computation.20 | convolution fusion | flops 3221225472 | bytes 17301508 | tf_op jit(solution)/shard_map/ajbk,bkl->ajbl/dot_general | solution.py:27
  43.0 7.7 gather_fusion
  50.7 8.6 %broadcast_select_fusion = f32[16,128,8,128]{1,3,2,0:T(8,128)} fusion(f32[16,128,8,128]{1,3,2,0:T(8,128)} %gather_fusion, pred[16]{0:T(512)(128)(4,1)S(1)} %compare_and_fusion), kind=kLoop, calls=%fused_computation.19 | loop fusion | flops 2097152 | bytes 16777232 | tf_op jit(solution)/shard_map/jit(_take)/select_n | solution.py:39
  59.3 7.7 gather_fusion.1
  67.0 8.1 copy.19
  75.1 7.0 bitcast_select_fusion
  82.2 174.8 %all-reduce.7.cloned.1.call-done = f32[2048,1024]{0,1:T(8,128)} async-done(((f32[2048,1024]{0,1:T(8,128)}), f32[2048,1024]{0,1:T(8,128)}) %all-reduce.7.cloned.1.call-update) | async-done | bytes 8388624 | tf_op jit(solution)/shard_map/psum | solution.py:41
  257.0 2.3 slice_select_fusion.4
  259.4 52.7 %all-reduce.9.cloned.1.call-done = f32[2048,128]{0,1:T(8,128)} async-done(((f32[2048,128]{0,1:T(8,128)}), f32[2048,128]{0,1:T(8,128)}) %all-reduce.9.cloned.1.call-update) | async-done | bytes 1048592 | tf_op jit(solution)/shard_map/psum | solution.py:12
  313.0 10.3 %all-gather.9.cloned.1.call-done = f32[4096,128]{0,1:T(8,128)} async-done(((f32[2048,128]{0,1:T(8,128)}), f32[4096,128]{0,1:T(8,128)}) %all-gather.9.cloned.1.call-update) | async-done | bytes 2097168 | tf_op jit(solution)/shard_map/all_gather | solution.py:51
  325.1 11.7 %cholesky.89 = f32[128,128]{1,0:T(8,128)S(1)} custom-call(f32[128,128]{1,0:T(8,128)S(1)} %fusion.38), custom_call_target="Cholesky" | custom-call | tf_op jit(solution)/shard_map/jit(cholesky)/cholesky | solution.py:52
  338.2 9.8 %custom-call.9 = f32[1,128,128]{1,2,0:T(8,128)S(1)} custom-call(f32[1,128,128]{2,1,0:T(8,128)S(1)} %fusion.24), custom_call_target="InvertDiagBlocksLowerTriangular" | custom-call | tf_op jit(solution)/shard_map/triangular_solve/custom-call.0 | solution.py:53
  348.0 3.5 convolution_bitcast_fusion.4
  351.5 9.4 %convolution_subtract_fusion.4 = f32[2048,1024]{0,1:T(8,128)S(1)} fusion(f32[2048,1024]{0,1:T(8,128)} %all-reduce.7.cloned.1.call-done, f32[4096,128]{0,1:T(8,128)S(1)} %convolution_bitcast_fusion.4, s32[]{:T(128)S(6)} %select_n.133, s32[]{:T(128)S(6)} %select_n.134), kind=kOutput, calls=%fused_computation.18 | convolution fusion | flops 3223322624 | bytes 18350088 | tf_op jit(solution)/shard_map/dot_general | solution.py:60
  361.9 3.4 copy-done
  365.2 1.1 slice_select_fusion.3
  366.4 53.2 %all-reduce.11.cloned.1.call-done = f32[2048,128]{0,1:T(8,128)} async-done(((f32[2048,128]{0,1:T(8,128)}), f32[2048,128]{0,1:T(8,128)}) %all-reduce.11.cloned.1.call-update) | async-done | bytes 1048592 | tf_op jit(solution)/shard_map/psum | solution.py:12
  419.6 1.1 compare_reduce_fusion.8
  420.7 10.1 %all-gather.11.cloned.1.call-done = f32[4096,128]{0,1:T(8,128)} async-done(((f32[2048,128]{0,1:T(8,128)}), f32[4096,128]{0,1:T(8,128)}) %all-gather.11.cloned.1.call-update) | async-done | bytes 2097168 | tf_op jit(solution)/shard_map/all_gather | solution.py:51
  432.6 11.7 %cholesky.100 = f32[128,128]{1,0:T(8,128)S(1)} custom-call(f32[128,128]{1,0:T(8,128)S(1)} %fusion.36), custom_call_target="Cholesky" | custom-call | tf_op jit(solution)/shard_map/jit(cholesky)/cholesky | solution.py:52
  445.7 9.8 %custom-call.10 = f32[1,128,128]{1,2,0:T(8,128)S(1)} custom-call(f32[1,128,128]{2,1,0:T(8,128)S(1)} %fusion.25), custom_call_target="InvertDiagBlocksLowerTriangular" | custom-call | tf_op jit(solution)/shard_map/triangular_solve/custom-call.0 | solution.py:53
  455.5 3.5 fusion.5
  459.0 9.4 %convolution_subtract_fusion.3 = f32[2048,1024]{0,1:T(8,128)S(1)} fusion(f32[2048,1024]{0,1:T(8,128)} %copy-done, f32[4096,128]{0,1:T(8,128)S(1)} %fusion.5, s32[]{:T(128)S(6)} %select_n.133, s32[]{:T(128)S(6)} %select_n.134), kind=kOutput, calls=%fused_computation.17 | convolution fusion | flops 3223322624 | bytes 18350088 | tf_op jit(solution)/shard_map/dot_general | solution.py:60
  469.3 3.4 copy-done.1
  473.8 53.2 %all-reduce.13.cloned.1.call-done = f32[2048,128]{0,1:T(8,128)} async-done(((f32[2048,128]{0,1:T(8,128)}), f32[2048,128]{0,1:T(8,128)}) %all-reduce.13.cloned.1.call-update) | async-done | bytes 1048592 | tf_op jit(solution)/shard_map/psum | solution.py:12
  527.9 10.6 %all-gather.13.cloned.1.call-done = f32[4096,128]{0,1:T(8,128)} async-done(((f32[2048,128]{0,1:T(8,128)}), f32[4096,128]{0,1:T(8,128)}) %all-gather.13.cloned.1.call-update) | async-done | bytes 2097168 | tf_op jit(solution)/shard_map/all_gather | solution.py:51
  540.2 11.7 %cholesky.111 = f32[128,128]{1,0:T(8,128)S(1)} custom-call(f32[128,128]{1,0:T(8,128)S(1)} %fusion.34), custom_call_target="Cholesky" | custom-call | tf_op jit(solution)/shard_map/jit(cholesky)/cholesky | solution.py:52
  553.2 9.8 %custom-call.11 = f32[1,128,128]{1,2,0:T(8,128)S(1)} custom-call(f32[1,128,128]{2,1,0:T(8,128)S(1)} %fusion.26), custom_call_target="InvertDiagBlocksLowerTriangular" | custom-call | tf_op jit(solution)/shard_map/triangular_solve/custom-call.0 | solution.py:53
  563.1 3.5 fusion.4
  566.6 9.4 %convolution_subtract_fusion.2 = f32[2048,1024]{0,1:T(8,128)S(1)} fusion(f32[2048,1024]{0,1:T(8,128)} %copy-done.1, f32[4096,128]{0,1:T(8,128)S(1)} %fusion.4, s32[]{:T(128)S(6)} %select_n.133, s32[]{:T(128)S(6)} %select_n.134), kind=kOutput, calls=%fused_computation.16 | convolution fusion | flops 3223322624 | bytes 18350088 | tf_op jit(solution)/shard_map/dot_general | solution.py:60
  576.9 3.4 copy-done.2
  581.8 52.8 %all-reduce.15.cloned.1.call-done = f32[2048,128]{0,1:T(8,128)} async-done(((f32[2048,128]{0,1:T(8,128)}), f32[2048,128]{0,1:T(8,128)}) %all-reduce.15.cloned.1.call-update) | async-done | bytes 1048592 | tf_op jit(solution)/shard_map/psum | solution.py:12
  635.3 10.6 %all-gather.15.cloned.1.call-done = f32[4096,128]{0,1:T(8,128)} async-done(((f32[2048,128]{0,1:T(8,128)}), f32[4096,128]{0,1:T(8,128)}) %all-gather.15.cloned.1.call-update) | async-done | bytes 2097168 | tf_op jit(solution)/shard_map/all_gather | solution.py:51
  647.6 11.7 %cholesky.122 = f32[128,128]{1,0:T(8,128)S(1)} custom-call(f32[128,128]{1,0:T(8,128)S(1)} %fusion.32), custom_call_target="Cholesky" | custom-call | tf_op jit(solution)/shard_map/jit(cholesky)/cholesky | solution.py:52
  660.7 9.8 %custom-call.12 = f32[1,128,128]{1,2,0:T(8,128)S(1)} custom-call(f32[1,128,128]{2,1,0:T(8,128)S(1)} %fusion.27), custom_call_target="InvertDiagBlocksLowerTriangular" | custom-call | tf_op jit(solution)/shard_map/triangular_solve/custom-call.0 | solution.py:53
  670.5 3.5 fusion.3
  674.0 9.4 %convolution_subtract_fusion.1 = f32[2048,1024]{0,1:T(8,128)S(1)} fusion(f32[2048,1024]{0,1:T(8,128)} %copy-done.2, f32[4096,128]{0,1:T(8,128)S(1)} %fusion.3, s32[]{:T(128)S(6)} %select_n.133, s32[]{:T(128)S(6)} %select_n.134), kind=kOutput, calls=%fused_computation.15 | convolution fusion | flops 3223322624 | bytes 18350088 | tf_op jit(solution)/shard_map/dot_general | solution.py:60
  684.3 3.4 copy-done.3
  689.0 53.0 %all-reduce.17.cloned.1.call-done = f32[2048,128]{0,1:T(8,128)} async-done(((f32[2048,128]{0,1:T(8,128)}), f32[2048,128]{0,1:T(8,128)}) %all-reduce.17.cloned.1.call-update) | async-done | bytes 1048592 | tf_op jit(solution)/shard_map/psum | solution.py:12
  742.7 10.6 %all-gather.17.cloned.1.call-done = f32[4096,128]{0,1:T(8,128)} async-done(((f32[2048,128]{0,1:T(8,128)}), f32[4096,128]{0,1:T(8,128)}) %all-gather.17.cloned.1.call-update) | async-done | bytes 2097168 | tf_op jit(solution)/shard_map/all_gather | solution.py:51
  755.1 11.7 %cholesky.133 = f32[128,128]{1,0:T(8,128)S(1)} custom-call(f32[128,128]{1,0:T(8,128)S(1)} %fusion.30), custom_call_target="Cholesky" | custom-call | tf_op jit(solution)/shard_map/jit(cholesky)/cholesky | solution.py:52
  768.1 9.8 %custom-call.13 = f32[1,128,128]{1,2,0:T(8,128)S(1)} custom-call(f32[1,128,128]{2,1,0:T(8,128)S(1)} %fusion.28), custom_call_target="InvertDiagBlocksLowerTriangular" | custom-call | tf_op jit(solution)/shard_map/triangular_solve/custom-call.0 | solution.py:53
  777.9 3.5 fusion.2
  781.5 11.2 %convolution_subtract_fusion = f32[2048,1024]{0,1:T(8,128)} fusion(f32[2048,1024]{0,1:T(8,128)} %copy-done.3, f32[4096,128]{0,1:T(8,128)S(1)} %fusion.2, s32[]{:T(128)S(6)} %select_n.133, s32[]{:T(128)S(6)} %select_n.134), kind=kOutput, calls=%fused_computation.14 | convolution fusion | flops 3223322624 | bytes 18350088 | tf_op jit(solution)/shard_map/dot_general | solution.py:60
  792.6 2.9 fusion.10
  795.5 9.2 %copy.30 = f32[2048,1024]{1,0:T(8,128)} copy(f32[2048,1024]{0,1:T(8,128)} %fusion.10) | data formatting | bytes 16777216 | tf_op jit(solution)/shard_map/scatter | solution.py:67
  (85 shorter events, 27.5 us)
Async XLA Ops:
  6.5 24.5 %all-gather.7.cloned.1.call-start = ((), (), s32[]{:S(2)}) async-start(), calls=%async_computation | async-start | bytes 3145728 | tf_op jit(solution)/shard_map/all_gather | solution.py:23
  7.3 249.7 %all-reduce.7.cloned.1.call-start = ((), (), s32[]{:S(2)}) async-start(), calls=%async_computation.1 | async-start | bytes 16777216 | tf_op jit(solution)/shard_map/psum | solution.py:41
  7.3 9.0 %copy-start.5 = (s32[1,32]{1,0:T(1,128)S(1)}, s32[1,32]{1,0:T(1,128)}, u32[]{:S(2)}) copy-start(s32[1,32]{1,0:T(1,128)} %param.18) | copy-start | bytes 388
  7.3 9.4 %copy-start.4 = (f32[1,16,128,128]{3,2,1,0:T(8,128)S(1)}, f32[1,16,128,128]{3,2,1,0:T(8,128)}, u32[]{:S(2)}) copy-start(f32[1,16,128,128]{3,2,1,0:T(8,128)} %param.17) | copy-start | bytes 3145732
  82.1 229.9 %all-reduce.9.cloned.1.call-start = ((), (), s32[]{:S(2)}) async-start(), calls=%async_computation.2 | async-start | bytes 2097152 | tf_op jit(solution)/shard_map/psum | solution.py:12
  259.3 64.0 %all-gather.9.cloned.1.call-start = ((), (), s32[]{:S(2)}) async-start(), calls=%async_computation.3 | async-start | bytes 3145728 | tf_op jit(solution)/shard_map/all_gather | solution.py:51
  312.1 107.5 %all-reduce.11.cloned.1.call-start = ((), (), s32[]{:S(2)}) async-start(), calls=%async_computation.4 | async-start | bytes 2097152 | tf_op jit(solution)/shard_map/psum | solution.py:12
  361.8 3.4 copy-start
  366.3 64.5 %all-gather.11.cloned.1.call-start = ((), (), s32[]{:S(2)}) async-start(), calls=%async_computation.5 | async-start | bytes 3145728 | tf_op jit(solution)/shard_map/all_gather | solution.py:51
  419.6 107.4 %all-reduce.13.cloned.1.call-start = ((), (), s32[]{:S(2)}) async-start(), calls=%async_computation.6 | async-start | bytes 2097152 | tf_op jit(solution)/shard_map/psum | solution.py:12
  469.3 3.4 copy-start.1
  473.8 64.6 %all-gather.13.cloned.1.call-start = ((), (), s32[]{:S(2)}) async-start(), calls=%async_computation.7 | async-start | bytes 3145728 | tf_op jit(solution)/shard_map/all_gather | solution.py:51
  527.0 107.6 %all-reduce.15.cloned.1.call-start = ((), (), s32[]{:S(2)}) async-start(), calls=%async_computation.8 | async-start | bytes 2097152 | tf_op jit(solution)/shard_map/psum | solution.py:12
  576.9 3.4 copy-start.2
  581.3 64.5 %all-gather.15.cloned.1.call-start = ((), (), s32[]{:S(2)}) async-start(), calls=%async_computation.9 | async-start | bytes 3145728 | tf_op jit(solution)/shard_map/all_gather | solution.py:51
  634.6 107.4 %all-reduce.17.cloned.1.call-start = ((), (), s32[]{:S(2)}) async-start(), calls=%async_computation.10 | async-start | bytes 2097152 | tf_op jit(solution)/shard_map/psum | solution.py:12
  684.3 3.4 copy-start.3
  688.8 64.5 %all-gather.17.cloned.1.call-start = ((), (), s32[]{:S(2)}) async-start(), calls=%async_computation.11 | async-start | bytes 3145728 | tf_op jit(solution)/shard_map/all_gather | solution.py:51
Sparse Core Ops, SparseCore 0:
  8.9 13.3 all-gather.6
  82.2 174.7 all-reduce.6
  259.4 52.5 all-reduce.8
  313.4 9.8 all-gather.8
  366.5 53.0 all-reduce.10
  421.0 9.8 all-gather.10
  473.9 53.0 all-reduce.12
  528.5 9.8 all-gather.12
  581.5 53.0 all-reduce.14
  636.0 9.8 all-gather.14
  688.9 53.0 all-reduce.16
  743.4 9.8 all-gather.16
where the time goes:
time: 821 us; the launch traced here: 812 us
  waiting for transfers between devices  493 us (60%)
  other arithmetic  151 us (18%)
  matrix products  92.7 us (11%)
  local copies, waits for them, and re-layouts  60 us (7%)
  between operations  14.1 us (2%)
    psum x5, waiting for transfers between devices, spread(): return lax.psum(block, axis)  265 us
    psum x1, waiting for transfers between devices, on_device(): matrix = lax.psum(rotated, 'grp')  175 us
    another operation x15, other arithmetic, on_device(): factor_block = jnp.linalg.cholesky(column[offset:offset + BLK])  62 us
    another operation x10, other arithmetic, on_device(): lax.linalg.triangular_solve(factor_block, column, left_side=False, lower=...  52.2 us
    all_gather x5, waiting for transfers between devices, on_device(): column = lax.all_gather(panel_piece, 'row', axis=0, tiled=True)  52.2 us
    dot_general x5, matrix products, on_device(): jnp.dot(own_rows, col_rows.T, precision=lax.Precision.HIGHEST, preferred_...  48.8 us
    unnamed x13, local copies, waits for them, and re-layouts  22.5 us
    another operation x5, matrix products, on_device(): lax.linalg.triangular_solve(factor_block, column, left_side=False, lower=...  17.5 us
  transfers between devices with their start and end apart: 12, of which 11 were waited for; matrix products, arithmetic and copies ran while one was open for 3% of the time, Pallas kernels for 0%

commit v1 on v0

--- a/solution.py
+++ b/solution.py
@@ -38,7 +38,9 @@
     )
     rotated = jnp.take(rotated, row_map, axis=0)
     rotated = jnp.take(rotated, col_map, axis=2).reshape(height, width)
-    matrix = lax.psum(rotated, "grp")
+    matrix = rotated
+    for hop in (1, 2):
+        matrix = matrix + lax.ppermute(matrix, "grp", [(dev, dev ^ hop) for dev in range(4)])
     row_offset = row_index * height
     own_count = matrix.shape[0]
     order_all = height * lax.axis_size("row")

time: 821 us -> 1040 us (1.27)
  waiting for transfers between devices: 493 us -> 680 us
  other arithmetic: 151 us -> 168 us
  matrix products: 92.7 us -> 104 us
    ppermute x0 -> x2, waiting for transfers between devices: none -> 361 us  [on_device(): lax.ppermute(matrix, 'grp', [(dev, dev ^ hop) for dev in range(4)])]
    psum x1 -> x0, waiting for transfers between devices: 175 us -> none  [on_device(): matrix = lax.psum(rotated, 'grp')]
    add x0 -> x2, other arithmetic: none -> 19.4 us  [on_device(): matrix + lax.ppermute(matrix, 'grp', [(dev, dev ^ hop) for dev in range(4)])]
    dot_general x1, matrix products: 12 us -> 23.6 us  [on_device(): jnp.einsum('ajbk,bkl->ajbl', half_done, col_transforms, precision=lax.Pre...]
  transfers between devices with their start and end apart: 12 -> 13, of which waited for: 11 -> 12; matrix products, arithmetic and copies ran while one was open for 3% -> 3% of each run, Pallas kernels for 0% -> 0%
where the time goes in v1:
time: 1040 us; the launch traced here: 1030 us
  waiting for transfers between devices  680 us (65%)
  other arithmetic  168 us (16%)
  matrix products  104 us (10%)
  local copies, waits for them, and re-layouts  60 us (6%)
  between operations  13.8 us (1%)
    ppermute x2, waiting for transfers between devices, on_device(): lax.ppermute(matrix, 'grp', [(dev, dev ^ hop) for dev in range(4)])  361 us
    psum x5, waiting for transfers between devices, spread(): return lax.psum(block, axis)  265 us
    another operation x15, other arithmetic, on_device(): factor_block = jnp.linalg.cholesky(column[offset:offset + BLK])  62 us
    all_gather x5, waiting for transfers between devices, on_device(): column = lax.all_gather(panel_piece, 'row', axis=0, tiled=True)  53 us
    another operation x10, other arithmetic, on_device(): lax.linalg.triangular_solve(factor_block, column, left_side=False, lower=...  52.2 us
    dot_general x5, matrix products, on_device(): jnp.dot(own_rows, col_rows.T, precision=lax.Precision.HIGHEST, preferred_...  48.8 us
    dot_general x1, matrix products, on_device(): jnp.einsum('ajbk,bkl->ajbl', half_done, col_transforms, precision=lax.Pre...  23.6 us
    unnamed x13, local copies, waits for them, and re-layouts  22.5 us
  transfers between devices with their start and end apart: 13, of which 12 were waited for; matrix products, arithmetic and copies ran while one was open for 3% of the time, Pallas kernels for 0%

profile of v1, /device:TPU:0, one launch (start us, length us, event | category | flops | bytes accessed | tf_op | source)
XLA Modules:
  0.0 1031.8 jit_solution(8755545976372448167)
XLA Ops:
  7.3 9.0 copy.38
  16.7 14.3 %fusion = f32[16,128,8,128]{3,1,0,2:T(8,128)} fusion(f32[16,128,8,128]{3,2,1,0:T(8,128)} %bitcast.112, f32[1,16,128,128]{3,2,1,0:T(8,128)S(1)} %copy-done.4), kind=kOutput, calls=%fused_computation.3 | convolution fusion | flops 3221225472 | bytes 17825792 | tf_op jit(solution)/shard_map/aij,aibk->ajbk/dot_general | solution.py:26
  31.0 23.6 %convolution_bitcast_fusion.5 = f32[16,128,8,128]{1,3,0,2:T(8,128)} fusion(f32[16,128,8,128]{3,1,0,2:T(8,128)} %fusion, f32[1,32,128,128]{3,2,0,1:T(8,128)} %all-gather.7.cloned.1.call-done, s32[]{:T(128)S(6)} %select_n.123), kind=kOutput, calls=%fused_computation.20 | convolution fusion | flops 3221225472 | bytes 17301508 | tf_op jit(solution)/shard_map/ajbk,bkl->ajbl/dot_general | solution.py:27
  54.6 7.7 gather_fusion
  62.3 8.6 broadcast_select_fusion
  70.8 7.7 gather_fusion.1
  78.5 8.1 copy.19
  86.7 4.8 bitcast_select_fusion
  91.5 3.1 collective-permute-start
  94.6 180.4 %collective-permute-done = f32[2048,1024]{0,1:T(8,128)S(1)} collective-permute-done((f32[2048,1024]{0,1:T(8,128)S(1)}, f32[2048,1024]{0,1:T(8,128)S(1)}, u32[]{:S(2)}, u32[]{:S(2)}) %collective-permute-start) | collective-permute-done | bytes 8388640 | tf_op jit(solution)/shard_map/ppermute | solution.py:43
  275.0 7.5 fusion.55
  284.3 180.1 %collective-permute-done.1 = f32[2048,1024]{0,1:T(8,128)} collective-permute-done((f32[2048,1024]{0,1:T(8,128)}, f32[2048,1024]{0,1:T(8,128)}, u32[]{:S(2)}, u32[]{:S(2)}) %collective-permute-start.1) | collective-permute-done | bytes 8388640 | tf_op jit(solution)/shard_map/ppermute | solution.py:43
  464.4 11.9 %add.92 = f32[2048,1024]{0,1:T(8,128)} add(f32[2048,1024]{0,1:T(8,128)} %fusion.55, f32[2048,1024]{0,1:T(8,128)} %collective-permute-done.1) | non-fusion elementwise | flops 2097152 | bytes 25165824 | tf_op jit(solution)/shard_map/add | solution.py:43
  478.7 53.3 %all-reduce.6.cloned.1.call-done = f32[2048,128]{0,1:T(8,128)} async-done(((f32[2048,128]{0,1:T(8,128)}), f32[2048,128]{0,1:T(8,128)}) %all-reduce.6.cloned.1.call-update) | async-done | bytes 1048592 | tf_op jit(solution)/shard_map/psum | solution.py:12
  533.1 10.3 %all-gather.9.cloned.1.call-done = f32[4096,128]{0,1:T(8,128)} async-done(((f32[2048,128]{0,1:T(8,128)}), f32[4096,128]{0,1:T(8,128)}) %all-gather.9.cloned.1.call-update) | async-done | bytes 2097168 | tf_op jit(solution)/shard_map/all_gather | solution.py:53
  545.2 11.7 %cholesky.89 = f32[128,128]{1,0:T(8,128)S(1)} custom-call(f32[128,128]{1,0:T(8,128)S(1)} %fusion.38), custom_call_target="Cholesky" | custom-call | tf_op jit(solution)/shard_map/jit(cholesky)/cholesky | solution.py:54
  558.3 9.8 custom-call.9
  568.1 3.5 convolution_bitcast_fusion.4
  571.6 9.4 convolution_subtract_fusion.4
  581.9 3.4 copy-done
  586.4 53.2 %all-reduce.8.cloned.1.call-done = f32[2048,128]{0,1:T(8,128)} async-done(((f32[2048,128]{0,1:T(8,128)}), f32[2048,128]{0,1:T(8,128)}) %all-reduce.8.cloned.1.call-update) | async-done | bytes 1048592 | tf_op jit(solution)/shard_map/psum | solution.py:12
  640.4 10.4 %all-gather.11.cloned.1.call-done = f32[4096,128]{0,1:T(8,128)} async-done(((f32[2048,128]{0,1:T(8,128)}), f32[4096,128]{0,1:T(8,128)}) %all-gather.11.cloned.1.call-update) | async-done | bytes 2097168 | tf_op jit(solution)/shard_map/all_gather | solution.py:53
  652.6 11.7 %cholesky.100 = f32[128,128]{1,0:T(8,128)S(1)} custom-call(f32[128,128]{1,0:T(8,128)S(1)} %fusion.36), custom_call_target="Cholesky" | custom-call | tf_op jit(solution)/shard_map/jit(cholesky)/cholesky | solution.py:54
  665.7 9.8 custom-call.10
  675.5 3.5 fusion.5
  679.0 9.4 convolution_subtract_fusion.3
  689.3 3.4 copy-done.1
  694.2 52.8 %all-reduce.10.cloned.1.call-done = f32[2048,128]{0,1:T(8,128)} async-done(((f32[2048,128]{0,1:T(8,128)}), f32[2048,128]{0,1:T(8,128)}) %all-reduce.10.cloned.1.call-update) | async-done | bytes 1048592 | tf_op jit(solution)/shard_map/psum | solution.py:12
  747.7 10.7 %all-gather.13.cloned.1.call-done = f32[4096,128]{0,1:T(8,128)} async-done(((f32[2048,128]{0,1:T(8,128)}), f32[4096,128]{0,1:T(8,128)}) %all-gather.13.cloned.1.call-update) | async-done | bytes 2097168 | tf_op jit(solution)/shard_map/all_gather | solution.py:53
  760.2 11.7 %cholesky.111 = f32[128,128]{1,0:T(8,128)S(1)} custom-call(f32[128,128]{1,0:T(8,128)S(1)} %fusion.34), custom_call_target="Cholesky" | custom-call | tf_op jit(solution)/shard_map/jit(cholesky)/cholesky | solution.py:54
  773.2 9.8 custom-call.11
  783.0 3.5 fusion.4
  786.6 9.4 convolution_subtract_fusion.2
  796.8 3.4 copy-done.2
  801.6 53.0 %all-reduce.12.cloned.1.call-done = f32[2048,128]{0,1:T(8,128)} async-done(((f32[2048,128]{0,1:T(8,128)}), f32[2048,128]{0,1:T(8,128)}) %all-reduce.12.cloned.1.call-update) | async-done | bytes 1048592 | tf_op jit(solution)/shard_map/psum | solution.py:12
  855.2 10.7 %all-gather.15.cloned.1.call-done = f32[4096,128]{0,1:T(8,128)} async-done(((f32[2048,128]{0,1:T(8,128)}), f32[4096,128]{0,1:T(8,128)}) %all-gather.15.cloned.1.call-update) | async-done | bytes 2097168 | tf_op jit(solution)/shard_map/all_gather | solution.py:53
  867.8 11.7 %cholesky.122 = f32[128,128]{1,0:T(8,128)S(1)} custom-call(f32[128,128]{1,0:T(8,128)S(1)} %fusion.32), custom_call_target="Cholesky" | custom-call | tf_op jit(solution)/shard_map/jit(cholesky)/cholesky | solution.py:54
  880.8 9.8 custom-call.12
  890.6 3.5 fusion.3
  894.1 9.4 convolution_subtract_fusion.1
  904.4 3.4 copy-done.3
  909.2 53.0 %all-reduce.14.cloned.1.call-done = f32[2048,128]{0,1:T(8,128)} async-done(((f32[2048,128]{0,1:T(8,128)}), f32[2048,128]{0,1:T(8,128)}) %all-reduce.14.cloned.1.call-update) | async-done | bytes 1048592 | tf_op jit(solution)/shard_map/psum | solution.py:12
  962.8 10.8 %all-gather.17.cloned.1.call-done = f32[4096,128]{0,1:T(8,128)} async-done(((f32[2048,128]{0,1:T(8,128)}), f32[4096,128]{0,1:T(8,128)}) %all-gather.17.cloned.1.call-update) | async-done | bytes 2097168 | tf_op jit(solution)/shard_map/all_gather | solution.py:53
  975.4 11.7 %cholesky.133 = f32[128,128]{1,0:T(8,128)S(1)} custom-call(f32[128,128]{1,0:T(8,128)S(1)} %fusion.30), custom_call_target="Cholesky" | custom-call | tf_op jit(solution)/shard_map/jit(cholesky)/cholesky | solution.py:54
  988.4 9.8 custom-call.13
  998.2 3.5 fusion.2
  1001.7 11.2 %convolution_subtract_fusion = f32[2048,1024]{0,1:T(8,128)} fusion(f32[2048,1024]{0,1:T(8,128)} %copy-done.3, f32[4096,128]{0,1:T(8,128)S(1)} %fusion.2, s32[]{:T(128)S(6)} %select_n.133, s32[]{:T(128)S(6)} %select_n.134), kind=kOutput, calls=%fused_computation.14 | convolution fusion | flops 3223322624 | bytes 18350088 | tf_op jit(solution)/shard_map/dot_general | solution.py:62
  1015.8 9.2 copy.30
  (88 shorter events, 36.3 us)
Async XLA Ops:
  6.5 24.5 %all-gather.7.cloned.1.call-start = ((), (), s32[]{:S(2)}) async-start(), calls=%async_computation | async-start | bytes 3145728 | tf_op jit(solution)/shard_map/all_gather | solution.py:23
  7.3 524.7 %all-reduce.6.cloned.1.call-start = ((), (), s32[]{:S(2)}) async-start(), calls=%async_computation.1 | async-start | bytes 2097152 | tf_op jit(solution)/shard_map/psum | solution.py:12
  7.3 9.0 copy-start.5
  7.3 9.4 copy-start.4
  91.5 183.5 %collective-permute-start = (f32[2048,1024]{0,1:T(8,128)S(1)}, f32[2048,1024]{0,1:T(8,128)S(1)}, u32[]{:S(2)}, u32[]{:S(2)}) collective-permute-start(f32[2048,1024]{0,1:T(8,128)S(1)} %bitcast_select_fusion), channel_id=1, source_target_pairs={{0,8},{8,0},{16,24},{24,16},{1,9},{9,1},{17,25},{25,17},{2,10},{10... | collective-permute-start | bytes 25165832 | tf_op jit(solution)/shard_map/ppermute | solution.py:43
  282.5 181.9 %collective-permute-start.1 = (f32[2048,1024]{0,1:T(8,128)}, f32[2048,1024]{0,1:T(8,128)}, u32[]{:S(2)}, u32[]{:S(2)}) collective-permute-start(f32[2048,1024]{0,1:T(8,128)} %fusion.55), channel_id=1, source_target_pairs={{0,16},{8,24},{16,0},{24,8},{1,17},{9,25},{17,1},{25,9},{2,18},{10... | collective-permute-start | bytes 25165832 | tf_op jit(solution)/shard_map/ppermute | solution.py:43
  478.6 64.8 %all-gather.9.cloned.1.call-start = ((), (), s32[]{:S(2)}) async-start(), calls=%async_computation.2 | async-start | bytes 3145728 | tf_op jit(solution)/shard_map/all_gather | solution.py:53
  532.0 107.5 %all-reduce.8.cloned.1.call-start = ((), (), s32[]{:S(2)}) async-start(), calls=%async_computation.3 | async-start | bytes 2097152 | tf_op jit(solution)/shard_map/psum | solution.py:12
  581.9 3.4 copy-start
  586.4 64.5 %all-gather.11.cloned.1.call-start = ((), (), s32[]{:S(2)}) async-start(), calls=%async_computation.4 | async-start | bytes 3145728 | tf_op jit(solution)/shard_map/all_gather | solution.py:53
  639.6 107.4 %all-reduce.10.cloned.1.call-start = ((), (), s32[]{:S(2)}) async-start(), calls=%async_computation.5 | async-start | bytes 2097152 | tf_op jit(solution)/shard_map/psum | solution.py:12
  689.3 3.4 copy-start.1
  693.8 64.6 %all-gather.13.cloned.1.call-start = ((), (), s32[]{:S(2)}) async-start(), calls=%async_computation.6 | async-start | bytes 3145728 | tf_op jit(solution)/shard_map/all_gather | solution.py:53
  747.0 107.5 %all-reduce.12.cloned.1.call-start = ((), (), s32[]{:S(2)}) async-start(), calls=%async_computation.7 | async-start | bytes 2097152 | tf_op jit(solution)/shard_map/psum | solution.py:12
  796.8 3.4 copy-start.2
  801.3 64.6 %all-gather.15.cloned.1.call-start = ((), (), s32[]{:S(2)}) async-start(), calls=%async_computation.8 | async-start | bytes 3145728 | tf_op jit(solution)/shard_map/all_gather | solution.py:53
  854.6 107.6 %all-reduce.14.cloned.1.call-start = ((), (), s32[]{:S(2)}) async-start(), calls=%async_computation.9 | async-start | bytes 2097152 | tf_op jit(solution)/shard_map/psum | solution.py:12
  904.4 3.4 copy-start.3
  908.9 64.7 %all-gather.17.cloned.1.call-start = ((), (), s32[]{:S(2)}) async-start(), calls=%async_computation.10 | async-start | bytes 3145728 | tf_op jit(solution)/shard_map/all_gather | solution.py:53
Sparse Core Ops, SparseCore 0:
  8.9 13.3 all-gather.6
  478.7 53.2 all-reduce.5
  533.5 9.8 all-gather.8
  586.5 53.0 all-reduce.7
  641.0 9.8 all-gather.10
  693.9 53.0 all-reduce.9
  748.5 9.8 all-gather.12
  801.5 53.0 all-reduce.11
  856.1 9.8 all-gather.14
  909.0 53.0 all-reduce.13
  963.7 9.8 all-gather.16
